TPU v7x, 32 devices: a whole 2x2x4 slice. The times are simulated.
32 devices in a mesh: head: 4 (over x, core), ctx: 8 (over z, y).
Axes of the slice: x: 2, y: 2, z: 4, core: 2. Of those that a mesh axis runs over, the one named last changes fastest.
Arguments:
- query: bfloat16 [8, 512, 512], P('ctx', 'head'), may hold values from -36 to 36
- key: bfloat16 [8, 512, 512], P('ctx', 'head'), may hold values from -36 to 36
- value: bfloat16 [8, 512, 512], P('ctx', 'head'), may hold values from -6 to 6
- resid_in: bfloat16 [8, 512, 1024], P('ctx', 'head'), may hold values from -6 to 6
- out_grad: bfloat16 [8, 512, 1024], P('ctx', 'head'), may hold values from -6 to 6
- out_weight: bfloat16 [512, 1024], replicated, may hold values from -0.25 to 0.25
- conv_kernel: bfloat16 [31, 1024], replicated, may hold values from -1 to 1
- frame_lengths: int32 [8], replicated, may hold values from 256 to 512, as said below
Outputs:
- d_resid: bfloat16 [8, 512, 1024], P('ctx', None, 'head')
- d_query: bfloat16 [8, 512, 512], P('ctx', None, 'head')
- d_key: bfloat16 [8, 512, 512], P('ctx', None, 'head')
- d_value: bfloat16 [8, 512, 512], P('ctx', None, 'head')
Inputs may be any that keep to these rules, and one draw needn't show every extreme that they name: Block b holds audio in its first frame_lengths[b] frames; at least one block is full.
All inputs are finite; a program needn't handle non-finite values.
Results may differ from a plain program's by a relative error of at most 0.0086.
Values may be sent and summed in bfloat16 or wider, within the bound.
No kernel may reach another device: no remote copies, remote signals or barrier semaphores. Data moves between devices by JAX's collectives and lax.ppermute only.
A program may use at most 128 MiB of HBM per device.

v0:
```python
import jax
import jax.numpy as jnp
from jax import lax
from jax.sharding import PartitionSpec as P

HEAD_DIM = 64
KERNEL = 31
REACH = 2


def padded(cells, sides, width):
    for axis, dim in sides:
        count = lax.axis_size(axis)
        ends = count - 1
        head = lax.slice_in_dim(cells, 0, width, axis=dim)
        tail = lax.slice_in_dim(cells, cells.shape[dim] - width, cells.shape[dim], axis=dim)
        cells = jnp.concatenate(
            [
                lax.ppermute(tail, axis, [(i, (i + 1) % count) for i in range(ends)]),
                cells,
                lax.ppermute(head, axis, [((i + 1) % count, i) for i in range(ends)]),
            ],
            axis=dim,
        )
    return cells


def shifted(value, axis, steps):
    count = lax.axis_size(axis)
    first, last = (max(0, -steps), min(count, count - steps))
    return lax.ppermute(value, axis, [(source, source + steps) for source in range(first, last)])


def swish_slope(before):
    logistic = jax.nn.sigmoid(before)
    return logistic * (1.0 + before * (1.0 - logistic))


def conv_backward(resid_wide, grad_wide, weights_here, frames_here):
    margin = (KERNEL - 1) // 2
    channels = resid_wide.shape[1]
    extent = frames_here + 2 * margin
    conv_pre = jnp.zeros((extent, channels), jnp.float32)
    for offset in range(KERNEL):
        conv_pre = conv_pre + weights_here[offset] * resid_wide[offset : offset + extent]
    conv_grad = grad_wide[margin : margin + extent] * swish_slope(conv_pre)
    total = grad_wide[2 * margin : 2 * margin + frames_here]
    for offset in range(KERNEL):
        start_at = 2 * margin - offset
        total = total + weights_here[offset] * conv_grad[start_at : start_at + frames_here]
    return total.astype(jnp.bfloat16)


def on_device(query, key, value, resid_in, out_grad, out_weight, conv_kernel, frame_lengths):
    margin = (KERNEL - 1) // 2
    reach_rows = 2 * margin
    head_place = lax.axis_index("head")
    moved = (
        lax.all_to_all(query, "head", split_axis=2, concat_axis=1, tiled=True),
        lax.all_to_all(key, "head", split_axis=2, concat_axis=1, tiled=True),
        lax.all_to_all(value, "head", split_axis=2, concat_axis=1, tiled=True),
        lax.all_to_all(resid_in, "head", split_axis=2, concat_axis=1, tiled=True),
        lax.all_to_all(out_grad, "head", split_axis=2, concat_axis=1, tiled=True),
    )
    query_rows = moved[0][0]
    key_rows = moved[1][0]
    value_rows = moved[2][0]
    resid_rows = moved[3][0]
    grad_rows = moved[4][0]
    block_frames = resid_rows.shape[0]
    channels = resid_rows.shape[1]
    weights_here = lax.dynamic_slice_in_dim(conv_kernel, head_place * channels, channels, 1).astype(
        jnp.float32
    )
    resid_ext, grad_ext = (
        padded(resid_rows, (("ctx", 0),), reach_rows),
        padded(grad_rows, (("ctx", 0),), reach_rows),
    )
    d_resid = conv_backward(
        resid_ext.astype(jnp.float32), grad_ext.astype(jnp.float32), weights_here, block_frames
    )
    width_cols = query_rows.shape[1]
    weight_rows = lax.dynamic_slice_in_dim(out_weight, head_place * width_cols, width_cols, 0)
    head_sum = lax.dot_general(
        lax.all_gather(d_resid, "head", axis=1, tiled=True),
        weight_rows,
        (((1,), (1,)), ((), ())),
        preferred_element_type=jnp.float32,
    )
    head_grad = head_sum.astype(jnp.bfloat16)
    d_resid_out = d_resid[None]
    frames_here = query_rows.shape[0]
    width_here = query_rows.shape[1]
    heads_here = width_here // HEAD_DIM
    scale = HEAD_DIM ** (-0.5)
    query_heads = query_rows.reshape(frames_here, heads_here, HEAD_DIM)
    grad_heads = head_grad.reshape(frames_here, heads_here, HEAD_DIM)
    block_place = lax.axis_index("ctx")
    block_count = frame_lengths.shape[0]
    window = REACH * frames_here
    local_rows = jnp.arange(frames_here, dtype=jnp.int32)
    query_place = block_place * frames_here + local_rows

    def live_mask(offset):
        neighbour = block_place + offset
        key_place = neighbour * frames_here + local_rows
        limit = frame_lengths[jnp.clip(neighbour, 0, block_count - 1)]
        inside = (neighbour >= 0) & (neighbour < block_count)
        near = jnp.abs(query_place[:, None] - key_place[None, :]) <= window
        return near & (local_rows[None, :] < limit) & inside

    fetched = {0: (key_rows, value_rows)}
    for direction in (1, -1):
        last_key, last_value = (key_rows, value_rows)
        for distance in range(1, REACH + 1):
            send_key = last_key
            send_value = last_value
            last_key, last_value = shifted((send_key, send_value), "ctx", direction)
            fetched[-direction * distance] = (last_key, last_value)
    order = [0] + [offset for offset in range(-REACH, REACH + 1) if offset != 0]

    def block_logits(offset):
        keys_now = fetched[offset][0].reshape(frames_here, heads_here, HEAD_DIM)
        raw = (
            jnp.einsum("qhd,khd->hqk", query_heads, keys_now, preferred_element_type=jnp.float32)
            * scale
        )
        return jnp.where(live_mask(offset)[None], raw, -jnp.inf)

    def block_slopes(offset):
        values_now = fetched[offset][1].reshape(frames_here, heads_here, HEAD_DIM)
        return jnp.einsum(
            "qhd,khd->hqk", grad_heads, values_now, preferred_element_type=jnp.float32
        )

    for offset in order:
        logits = block_logits(offset)
        slopes = block_slopes(offset)
        if offset == 0:
            highest = jnp.max(logits, axis=2)
            scaled = jnp.exp(logits - highest[:, :, None])
            mass = jnp.sum(scaled, axis=2)
            weighted = jnp.sum(scaled * slopes, axis=2)
        else:
            fresh = jnp.maximum(highest, jnp.max(logits, axis=2))
            factor = jnp.exp(highest - fresh)
            scaled = jnp.exp(logits - fresh[:, :, None])
            mass = mass * factor + jnp.sum(scaled, axis=2)
            weighted = weighted * factor + jnp.sum(scaled * slopes, axis=2)
            highest = fresh
    log_total = highest + jnp.log(mass)
    delta = weighted / mass
    query_grad = jnp.zeros((frames_here, heads_here, HEAD_DIM), jnp.float32)
    for offset in order:
        keys_now = fetched[offset][0].reshape(frames_here, heads_here, HEAD_DIM)
        logits = block_logits(offset)
        probs = jnp.exp(logits - log_total[:, :, None])
        slopes = block_slopes(offset)
        dlogits = (probs * (slopes - delta[:, :, None])).astype(jnp.bfloat16)
        probs_low = probs.astype(jnp.bfloat16)
        query_grad = (
            query_grad
            + jnp.einsum("hqk,khd->qhd", dlogits, keys_now, preferred_element_type=jnp.float32)
            * scale
        )
        key_part = (
            (
                jnp.einsum("hqk,qhd->khd", dlogits, query_heads, preferred_element_type=jnp.float32)
                * scale
            )
            .astype(jnp.bfloat16)
            .reshape(frames_here, width_here)
        )
        value_part = (
            jnp.einsum("hqk,qhd->khd", probs_low, grad_heads, preferred_element_type=jnp.float32)
            .astype(jnp.bfloat16)
            .reshape(frames_here, width_here)
        )
        if offset == 0:
            key_total = key_part.astype(jnp.float32)
            value_total = value_part.astype(jnp.float32)
        else:
            back_key, back_value = shifted((key_part, value_part), "ctx", offset)
            key_total = key_total + back_key.astype(jnp.float32)
            value_total = value_total + back_value.astype(jnp.float32)
    return (
        d_resid_out,
        query_grad.reshape(frames_here, width_here).astype(jnp.bfloat16)[None],
        key_total.astype(jnp.bfloat16)[None],
        value_total.astype(jnp.bfloat16)[None],
    )


def solution(mesh):
    in_specs = (
        P("ctx", "head", None),
        P("ctx", "head", None),
        P("ctx", "head", None),
        P("ctx", "head", None),
        P("ctx", "head", None),
        P(),
        P(),
        P(),
    )
    out_specs = (
        P("ctx", None, "head"),
        P("ctx", None, "head"),
        P("ctx", None, "head"),
        P("ctx", None, "head"),
    )
    return jax.shard_map(
        on_device, mesh=mesh, in_specs=in_specs, out_specs=out_specs, check_vma=False
    )
```

profile of v0, /device:TPU:14, one launch (start us, length us, event | category | flops | bytes accessed | tf_op | source)
XLA Modules:
  0.0 204.8 jit_solution(15611372679468310429)
XLA Ops:
  11.0 3.8 %all-to-all-start.2 = ((bf16[4,2,8192]{2,1,0:T(2,128)(2,1)}), bf16[4,2,8192]{2,1,0:T(2,128)(2,1)S(1)}, u32[]{:S(2)}, u32[]{:S(2)}) async-start(bf16[4,2,8192]{2,1,0:T(2,128)(2,1)} %reshape.507), calls=%async_computation.2 | async-start | bytes 262144 | tf_op jit(solution)/shard_map/all_to_all | solution.py:59
  19.6 3.0 %fusion.33 = (pred[512,512]{0,1:T(8,128)(4,1)}, pred[512,512]{0,1:T(8,128)(4,1)}, pred[512,512]{0,1:T(8,128)(4,1)}, pred[512,512]{0,1:T(8,128)(4,1)}, pred[512,512]{0,1:T(8,128)(4,1)}) fusion(s32[512]{0:T(512)S(1)} %get-tuple-element.108, s32[512]{0:T(512)S(1)} %iota_add_fusion.4, pred[512]{0:T(512)(128)(4,1)S(1)} %get-tuple-element.106, pred[]{:T(512)S(6)} %and.169, ...), kind=kLoop, calls=%fused_computation.72 | loop fusion | flops 6553600 | bytes 1323525 | tf_op jit(solution)/shard_map/and | solution.py:110
  27.2 3.4 %all-to-all-start.3 = ((bf16[4,2,8192]{2,1,0:T(2,128)(2,1)}), bf16[4,2,8192]{2,1,0:T(2,128)(2,1)S(1)}, u32[]{:S(2)}, u32[]{:S(2)}) async-start(bf16[4,2,8192]{2,1,0:T(2,128)(2,1)} %reshape.503), calls=%async_computation.3 | async-start | bytes 262144 | tf_op jit(solution)/shard_map/all_to_all | solution.py:60
  31.3 2.2 %all-to-all-done.3 = bf16[4,2,8192]{2,1,0:T(2,128)(2,1)S(1)} async-done(((bf16[4,2,8192]{2,1,0:T(2,128)(2,1)}), bf16[4,2,8192]{2,1,0:T(2,128)(2,1)S(1)}, u32[]{:S(2)}, u32[]{:S(2)}) %all-to-all-start.3) | async-done | bytes 131104 | tf_op jit(solution)/shard_map/all_to_all | solution.py:60
  33.5 5.0 %all-to-all-start.4 = ((bf16[4,2,8192]{2,1,0:T(2,128)(2,1)}), bf16[4,2,8192]{2,1,0:T(2,128)(2,1)S(1)}, u32[]{:S(2)}, u32[]{:S(2)}) async-start(bf16[4,2,8192]{2,1,0:T(2,128)(2,1)} %reshape.505), calls=%async_computation.4 | async-start | bytes 262144 | tf_op jit(solution)/shard_map/all_to_all | solution.py:61
  38.9 2.2 %reduce.1 = bf16[1024,128]{1,0:T(8,128)(2,1)S(1)} reduce(bf16[1024,1,128]{2,1,0:T(2,128)(2,1)S(1)} %bitcast.177, bf16[]{:T(256)} %broadcast.279), dimensions={1}, to_apply=%bitcast.110.reduce_sub_computation | reduce | bytes 524290
  42.3 2.2 %reduce = bf16[1024,128]{1,0:T(8,128)(2,1)S(1)} reduce(bf16[1024,1,128]{2,1,0:T(2,128)(2,1)S(1)} %bitcast.176, bf16[]{:T(256)} %broadcast.279), dimensions={1}, to_apply=%bitcast.108.reduce_sub_computation | reduce | bytes 524290
  45.3 3.4 %all-to-all-start.1 = ((bf16[4,2,16384]{2,1,0:T(2,128)(2,1)}), bf16[4,2,16384]{2,1,0:T(2,128)(2,1)S(1)}, u32[]{:S(2)}, u32[]{:S(2)}) async-start(bf16[4,2,16384]{2,1,0:T(2,128)(2,1)} %reshape.501), calls=%async_computation.1 | async-start | bytes 524288 | tf_op jit(solution)/shard_map/all_to_all | solution.py:62
  49.7 2.4 %collective-permute-start.6 = (bf16[512,128]{1,0:T(8,128)(2,1)}, bf16[512,128]{1,0:T(8,128)(2,1)}, u32[]{:S(2)}, u32[]{:S(2)}) collective-permute-start(bf16[512,128]{1,0:T(8,128)(2,1)} %bitcast.40), channel_id=1, source_target_pairs={{1,0},{2,1},{3,2},{4,3},{5,4},{6,5},{7,6},{9,8},{10,9},{11,10},{12... | collective-permute-start | bytes 393224 | tf_op jit(solution)/shard_map/ppermute | solution.py:31
  52.2 4.3 %collective-permute-start.4 = (bf16[512,128]{1,0:T(8,128)(2,1)}, bf16[512,128]{1,0:T(8,128)(2,1)}, u32[]{:S(2)}, u32[]{:S(2)}) collective-permute-start(bf16[512,128]{1,0:T(8,128)(2,1)} %bitcast.40), channel_id=1, source_target_pairs={{0,1},{1,2},{2,3},{3,4},{4,5},{5,6},{6,7},{8,9},{9,10},{10,11},{11... | collective-permute-start | bytes 393224 | tf_op jit(solution)/shard_map/ppermute | solution.py:31
  57.8 1.9 collective-permute-start.10
  59.8 3.4 %all-to-all-start = ((bf16[4,2,16384]{2,1,0:T(2,128)(2,1)}), bf16[4,2,16384]{2,1,0:T(2,128)(2,1)S(1)}, u32[]{:S(2)}, u32[]{:S(2)}) async-start(bf16[4,2,16384]{2,1,0:T(2,128)(2,1)} %reshape.499), calls=%async_computation | async-start | bytes 524288 | tf_op jit(solution)/shard_map/all_to_all | solution.py:63
  63.7 4.8 %collective-permute-start.2 = (bf16[30,256]{1,0:T(8,128)(2,1)S(1)}, bf16[30,256]{1,0:T(8,128)(2,1)S(1)}, u32[]{:S(2)}, u32[]{:S(2)}) collective-permute-start(bf16[30,256]{1,0:T(8,128)(2,1)S(1)} %get-tuple-element.36), channel_id=1, source_target_pairs={{0,1},{1,2},{2,3},{3,4},{4,5},{5,6},{6,7},{8,9},{9,10},{10,11},{11... | collective-permute-start | bytes 46088 | tf_op jit(solution)/shard_map/ppermute | solution.py:19
  68.6 1.9 collective-permute-start.3
  71.0 4.8 %collective-permute-start = (bf16[30,256]{1,0:T(8,128)(2,1)S(1)}, bf16[30,256]{1,0:T(8,128)(2,1)S(1)}, u32[]{:S(2)}, u32[]{:S(2)}) collective-permute-start(bf16[30,256]{1,0:T(8,128)(2,1)S(1)} %get-tuple-element.38), channel_id=1, source_target_pairs={{0,1},{1,2},{2,3},{3,4},{4,5},{5,6},{6,7},{8,9},{9,10},{10,11},{11... | collective-permute-start | bytes 46088 | tf_op jit(solution)/shard_map/ppermute | solution.py:19
  75.8 1.9 collective-permute-start.1
  77.9 5.0 %collective-permute-start.8 = (bf16[512,128]{1,0:T(8,128)(2,1)}, bf16[512,128]{1,0:T(8,128)(2,1)}, u32[]{:S(2)}, u32[]{:S(2)}) collective-permute-start(bf16[512,128]{1,0:T(8,128)(2,1)} %bitcast.50), channel_id=1, source_target_pairs={{0,1},{1,2},{2,3},{3,4},{4,5},{5,6},{6,7},{8,9},{9,10},{10,11},{11... | collective-permute-start | bytes 393224 | tf_op jit(solution)/shard_map/ppermute | solution.py:31
  82.9 2.4 %slice_multiply_fusion.31 = f32[542,256]{1,0:T(8,128)S(1)} fusion(f32[572,256]{1,0:T(8,128)S(1)} %maximum_convert_fusion, f32[572,256]{1,0:T(8,128)S(1)} %maximum_convert_fusion.1, f32[256]{0:T(256)S(1)} %bitcast.221, f32[256]{0:T(256)S(1)} %bitcast.223, f32[256]{0:T(256)S(1)} %bitcast.225, f32[256]{0:T(256)S(1)} %bitcast.227, f32[256]{0:T(256)S(1)} %bitcast.229, ...), kind=kLoop, calls=%fused_computation.140 | loop fusion | flops 9573888 | bytes 18347008 | tf_op jit(solution)/shard_map/mul | solution.py:46
  85.4 2.8 %fusion.71 = bf16[512,256]{1,0:T(8,128)(2,1)} fusion(f32[542,256]{1,0:T(8,128)S(1)} %slice_multiply_fusion.31, f32[572,256]{1,0:T(8,128)S(1)} %maximum_convert_fusion, f32[256]{0:T(256)S(1)} %bitcast.222, f32[256]{0:T(256)S(1)} %bitcast.224, f32[256]{0:T(256)S(1)} %bitcast.226, f32[256]{0:T(256)S(1)} %bitcast.228, f32[256]{0:T(256)S(1)} %bitcast.230, ...), kind=kLoop, calls=%fused_computation.143 | loop fusion | flops 8257536 | bytes 17071104 | tf_op jit(solution)/shard_map/convert_element_type | solution.py:51
  91.0 1.9 collective-permute-start.7
  92.9 1.7 copy.123
  94.6 4.9 %collective-permute-start.5 = (bf16[512,128]{1,0:T(8,128)(2,1)}, bf16[512,128]{1,0:T(8,128)(2,1)}, u32[]{:S(2)}, u32[]{:S(2)}) collective-permute-start(bf16[512,128]{1,0:T(8,128)(2,1)} %collective-permute-done.4), channel_id=1, source_target_pairs={{0,1},{1,2},{2,3},{3,4},{4,5},{5,6},{6,7},{8,9},{9,10},{10,11},{11... | collective-permute-start | bytes 393224 | tf_op jit(solution)/shard_map/ppermute | solution.py:31
  99.6 1.9 collective-permute-start.11
  101.5 4.8 %collective-permute-start.9 = (bf16[512,128]{1,0:T(8,128)(2,1)}, bf16[512,128]{1,0:T(8,128)(2,1)}, u32[]{:S(2)}, u32[]{:S(2)}) collective-permute-start(bf16[512,128]{1,0:T(8,128)(2,1)} %collective-permute-done.8), channel_id=1, source_target_pairs={{0,1},{1,2},{2,3},{3,4},{4,5},{5,6},{6,7},{8,9},{9,10},{10,11},{11... | collective-permute-start | bytes 393224 | tf_op jit(solution)/shard_map/ppermute | solution.py:31
  106.4 3.5 %fusion.113 = (f32[2,512]{1,0:T(2,128)}, f32[2,512,512]{1,2,0:T(8,128)}) fusion(bf16[512,2,64]{0,2,1:T(8,128)(2,1)S(1)} %reshape_squeeze.12, bf16[512,2,64]{0,2,1:T(8,128)(2,1)S(1)} %bitcast.213, pred[512,512]{0,1:T(8,128)(4,1)} %get-tuple-element.78), kind=kOutput, calls=%fused_computation.237 | convolution fusion | flops 68680704 | bytes 2625536 | tf_op jit(solution)/shard_map/qhd,khd->hqk/dot_general | solution.py:125
  109.9 2.5 %fusion.114 = (f32[2,512]{1,0:T(2,128)}, f32[2,512,512]{1,2,0:T(8,128)}) fusion(bf16[512,2,64]{0,2,1:T(8,128)(2,1)S(1)} %reshape_squeeze.12, bf16[512,2,64]{0,2,1:T(8,128)(2,1)S(1)} %bitcast.217, pred[512,512]{0,1:T(8,128)(4,1)S(1)} %copy-done.27), kind=kOutput, calls=%fused_computation.238 | convolution fusion | flops 68680704 | bytes 2625536 | tf_op jit(solution)/shard_map/qhd,khd->hqk/dot_general | solution.py:125
  112.4 1.7 copy.131
  116.7 1.7 copy.122
  118.4 1.7 copy.132
  120.1 1.7 copy.129
  121.8 3.0 %fusion.116 = (f32[2,512]{1,0:T(2,128)S(1)}, f32[2,512,512]{1,2,0:T(8,128)}) fusion(bf16[512,2,64]{0,2,1:T(8,128)(2,1)S(1)} %reshape_squeeze.12, bf16[512,2,64]{0,2,1:T(8,128)(2,1)} %bitcast.215, pred[512,512]{0,1:T(8,128)(4,1)} %get-tuple-element.76), kind=kOutput, calls=%fused_computation.240 | convolution fusion | flops 68680704 | bytes 2625536 | tf_op jit(solution)/shard_map/qhd,khd->hqk/dot_general | solution.py:125
  124.8 2.0 fusion.112
  126.9 1.7 convolution_convert_fusion.5
  140.7 4.3 %multiply_convert_fusion = (bf16[2,512,512]{1,2,0:T(8,128)(2,1)}, bf16[2,512,512]{1,2,0:T(8,128)(2,1)}, bf16[2,512,512]{1,2,0:T(8,128)(2,1)}, bf16[2,512,512]{1,2,0:T(8,128)(2,1)S(1)}, bf16[2,512,512]{1,2,0:T(8,128)(2,1)}) fusion(f32[2,512,512]{1,2,0:T(8,128)S(1)} %get-tuple-element.96, f32[2,512,512]{1,2,0:T(8,128)S(1)} %copy-done.4, ...), kind=kLoop, calls=%fused_computation | loop fusion | flops 10485760 | bytes 26222592 | tf_op jit(solution)/shard_map/convert_element_type | solution.py:159
  151.5 1.7 copy.147
  153.2 2.3 %fusion.15 = bf16[2,512,64]{1,2,0:T(8,128)(2,1)} fusion(bf16[2,512,512]{1,2,0:T(8,128)(2,1)} %get-tuple-element.72, bf16[512,2,64]{0,2,1:T(8,128)(2,1)S(1)} %reshape_squeeze.12), kind=kOutput, calls=%fused_computation.54 | convolution fusion | flops 67239936 | bytes 1310720 | tf_op jit(solution)/shard_map/hqk,qhd->khd/dot_general | solution.py:168
  157.2 2.3 %fusion.16 = bf16[2,512,64]{1,2,0:T(8,128)(2,1)} fusion(bf16[2,512,512]{1,2,0:T(8,128)(2,1)} %get-tuple-element.73, bf16[512,2,64]{0,2,1:T(8,128)(2,1)S(1)} %reshape_squeeze.12), kind=kOutput, calls=%fused_computation.55 | convolution fusion | flops 67239936 | bytes 1310720 | tf_op jit(solution)/shard_map/hqk,qhd->khd/dot_general | solution.py:168
  161.1 1.7 copy.145
  167.1 1.7 copy.158
  168.7 2.0 collective-permute-start.14
  170.8 3.8 %collective-permute-start.13 = (bf16[512,128]{1,0:T(8,128)(2,1)}, bf16[512,128]{1,0:T(8,128)(2,1)S(1)}, u32[]{:S(2)}, u32[]{:S(2)}) collective-permute-start(bf16[512,128]{1,0:T(8,128)(2,1)} %copy.143), channel_id=1, source_target_pairs={{1,0},{2,1},{3,2},{4,3},{5,4},{6,5},{7,6},{9,8},{10,9},{11,10},{12... | collective-permute-start | bytes 393224 | tf_op jit(solution)/shard_map/ppermute | solution.py:31
  174.6 2.4 %collective-permute-start.12 = (bf16[512,128]{1,0:T(8,128)(2,1)}, bf16[512,128]{1,0:T(8,128)(2,1)S(1)}, u32[]{:S(2)}, u32[]{:S(2)}) collective-permute-start(bf16[512,128]{1,0:T(8,128)(2,1)} %copy.140), channel_id=1, source_target_pairs={{2,0},{3,1},{4,2},{5,3},{6,4},{7,5},{10,8},{11,9},{12,10},{13,11},... | collective-permute-start | bytes 393224 | tf_op jit(solution)/shard_map/ppermute | solution.py:31
  177.0 3.5 %collective-permute-start.15 = (bf16[512,128]{1,0:T(8,128)(2,1)}, bf16[512,128]{1,0:T(8,128)(2,1)S(1)}, u32[]{:S(2)}, u32[]{:S(2)}) collective-permute-start(bf16[512,128]{1,0:T(8,128)(2,1)} %copy.147), channel_id=1, source_target_pairs={{0,2},{1,3},{2,4},{3,5},{4,6},{5,7},{8,10},{9,11},{10,12},{11,13},... | collective-permute-start | bytes 393224 | tf_op jit(solution)/shard_map/ppermute | solution.py:31
  181.0 2.4 %collective-permute-start.16 = (bf16[512,128]{1,0:T(8,128)(2,1)}, bf16[512,128]{1,0:T(8,128)(2,1)S(1)}, u32[]{:S(2)}, u32[]{:S(2)}) collective-permute-start(bf16[512,128]{1,0:T(8,128)(2,1)} %copy.150), channel_id=1, source_target_pairs={{2,0},{3,1},{4,2},{5,3},{6,4},{7,5},{10,8},{11,9},{12,10},{13,11},... | collective-permute-start | bytes 393224 | tf_op jit(solution)/shard_map/ppermute | solution.py:31
  183.4 1.9 collective-permute-start.17
  185.3 4.8 %collective-permute-start.18 = (bf16[512,128]{1,0:T(8,128)(2,1)}, bf16[512,128]{1,0:T(8,128)(2,1)S(1)}, u32[]{:S(2)}, u32[]{:S(2)}) collective-permute-start(bf16[512,128]{1,0:T(8,128)(2,1)} %copy.155), channel_id=1, source_target_pairs={{0,1},{1,2},{2,3},{3,4},{4,5},{5,6},{6,7},{8,9},{9,10},{10,11},{11... | collective-permute-start | bytes 393224 | tf_op jit(solution)/shard_map/ppermute | solution.py:31
  190.2 3.5 %collective-permute-start.19 = (bf16[512,128]{1,0:T(8,128)(2,1)}, bf16[512,128]{1,0:T(8,128)(2,1)S(1)}, u32[]{:S(2)}, u32[]{:S(2)}) collective-permute-start(bf16[512,128]{1,0:T(8,128)(2,1)} %copy.157), channel_id=1, source_target_pairs={{0,2},{1,3},{2,4},{3,5},{4,6},{5,7},{8,10},{9,11},{10,12},{11,13},... | collective-permute-start | bytes 393224 | tf_op jit(solution)/shard_map/ppermute | solution.py:31
  194.4 2.8 %collective-permute-done.19 = bf16[512,128]{1,0:T(8,128)(2,1)S(1)} collective-permute-done((bf16[512,128]{1,0:T(8,128)(2,1)}, bf16[512,128]{1,0:T(8,128)(2,1)S(1)}, u32[]{:S(2)}, u32[]{:S(2)}) %collective-permute-start.19) | collective-permute-done | bytes 131104 | tf_op jit(solution)/shard_map/ppermute | solution.py:31
  (177 shorter events, 53.0 us)
Async XLA Ops:
  7.2 119.7 %copy-start = (bf16[512,1024]{1,0:T(8,128)(2,1)S(1)}, bf16[512,1024]{1,0:T(8,128)(2,1)}, u32[]{:S(2)}) copy-start(bf16[512,1024]{1,0:T(8,128)(2,1)} %param.13) | copy-start | bytes 3145732
  7.2 15.4 %copy-start.28 = (bf16[1,128,512]{2,1,0:T(8,128)(2,1)S(1)}, bf16[1,128,512]{2,1,0:T(8,128)(2,1)}, u32[]{:S(2)}) copy-start(bf16[1,128,512]{2,1,0:T(8,128)(2,1)} %param.9) | copy-start | bytes 393220
  7.2 17.7 %copy-start.29 = (bf16[1,128,512]{2,1,0:T(8,128)(2,1)S(1)}, bf16[1,128,512]{2,1,0:T(8,128)(2,1)}, u32[]{:S(2)}) copy-start(bf16[1,128,512]{2,1,0:T(8,128)(2,1)} %param.10) | copy-start | bytes 393220
  11.0 16.2 %all-to-all-start.2 = ((bf16[4,2,8192]{2,1,0:T(2,128)(2,1)}), bf16[4,2,8192]{2,1,0:T(2,128)(2,1)S(1)}, u32[]{:S(2)}, u32[]{:S(2)}) async-start(bf16[4,2,8192]{2,1,0:T(2,128)(2,1)} %reshape.507), calls=%async_computation.2 | async-start | bytes 262144 | tf_op jit(solution)/shard_map/all_to_all | solution.py:59
  14.8 23.7 %copy-start.24 = (bf16[1,128,1024]{2,1,0:T(8,128)(2,1)S(1)}, bf16[1,128,1024]{2,1,0:T(8,128)(2,1)}, u32[]{:S(2)}) copy-start(bf16[1,128,1024]{2,1,0:T(8,128)(2,1)} %param.11) | copy-start | bytes 786436
  24.2 17.7 %copy-start.25 = (bf16[1,128,1024]{2,1,0:T(8,128)(2,1)S(1)}, bf16[1,128,1024]{2,1,0:T(8,128)(2,1)}, u32[]{:S(2)}) copy-start(bf16[1,128,1024]{2,1,0:T(8,128)(2,1)} %param.12) | copy-start | bytes 786436
  27.2 6.4 %all-to-all-start.3 = ((bf16[4,2,8192]{2,1,0:T(2,128)(2,1)}), bf16[4,2,8192]{2,1,0:T(2,128)(2,1)S(1)}, u32[]{:S(2)}, u32[]{:S(2)}) async-start(bf16[4,2,8192]{2,1,0:T(2,128)(2,1)} %reshape.503), calls=%async_computation.3 | async-start | bytes 262144 | tf_op jit(solution)/shard_map/all_to_all | solution.py:60
  33.5 11.8 %all-to-all-start.4 = ((bf16[4,2,8192]{2,1,0:T(2,128)(2,1)}), bf16[4,2,8192]{2,1,0:T(2,128)(2,1)S(1)}, u32[]{:S(2)}, u32[]{:S(2)}) async-start(bf16[4,2,8192]{2,1,0:T(2,128)(2,1)} %reshape.505), calls=%async_computation.4 | async-start | bytes 262144 | tf_op jit(solution)/shard_map/all_to_all | solution.py:61
  45.3 14.5 %all-to-all-start.1 = ((bf16[4,2,16384]{2,1,0:T(2,128)(2,1)}), bf16[4,2,16384]{2,1,0:T(2,128)(2,1)S(1)}, u32[]{:S(2)}, u32[]{:S(2)}) async-start(bf16[4,2,16384]{2,1,0:T(2,128)(2,1)} %reshape.501), calls=%async_computation.1 | async-start | bytes 524288 | tf_op jit(solution)/shard_map/all_to_all | solution.py:62
  49.7 40.2 %collective-permute-start.6 = (bf16[512,128]{1,0:T(8,128)(2,1)}, bf16[512,128]{1,0:T(8,128)(2,1)}, u32[]{:S(2)}, u32[]{:S(2)}) collective-permute-start(bf16[512,128]{1,0:T(8,128)(2,1)} %bitcast.40), channel_id=1, source_target_pairs={{1,0},{2,1},{3,2},{4,3},{5,4},{6,5},{7,6},{9,8},{10,9},{11,10},{12... | collective-permute-start | bytes 393224 | tf_op jit(solution)/shard_map/ppermute | solution.py:31
  52.2 40.8 %collective-permute-start.4 = (bf16[512,128]{1,0:T(8,128)(2,1)}, bf16[512,128]{1,0:T(8,128)(2,1)}, u32[]{:S(2)}, u32[]{:S(2)}) collective-permute-start(bf16[512,128]{1,0:T(8,128)(2,1)} %bitcast.40), channel_id=1, source_target_pairs={{0,1},{1,2},{2,3},{3,4},{4,5},{5,6},{6,7},{8,9},{9,10},{10,11},{11... | collective-permute-start | bytes 393224 | tf_op jit(solution)/shard_map/ppermute | solution.py:31
  56.9 31.3 %copy-start.19 = (bf16[512,2,64]{0,2,1:T(8,128)(2,1)}, bf16[512,2,64]{0,2,1:T(8,128)(2,1)S(1)}, u32[]{:S(2)}) copy-start(bf16[512,2,64]{0,2,1:T(8,128)(2,1)S(1)} %reshape_squeeze.13) | copy-start | bytes 393220
  57.8 41.7 %collective-permute-start.10 = (bf16[512,128]{1,0:T(8,128)(2,1)}, bf16[512,128]{1,0:T(8,128)(2,1)}, u32[]{:S(2)}, u32[]{:S(2)}) collective-permute-start(bf16[512,128]{1,0:T(8,128)(2,1)} %bitcast.50), channel_id=1, source_target_pairs={{1,0},{2,1},{3,2},{4,3},{5,4},{6,5},{7,6},{9,8},{10,9},{11,10},{12... | collective-permute-start | bytes 393224 | tf_op jit(solution)/shard_map/ppermute | solution.py:31
  59.8 10.7 %all-to-all-start = ((bf16[4,2,16384]{2,1,0:T(2,128)(2,1)}), bf16[4,2,16384]{2,1,0:T(2,128)(2,1)S(1)}, u32[]{:S(2)}, u32[]{:S(2)}) async-start(bf16[4,2,16384]{2,1,0:T(2,128)(2,1)} %reshape.499), calls=%async_computation | async-start | bytes 524288 | tf_op jit(solution)/shard_map/all_to_all | solution.py:63
  63.2 63.7 %all-gather.2.cloned.1.call-start = ((), (), s32[]{:S(2)}) async-start(), calls=%async_computation.5 | async-start | bytes 1310720 | tf_op jit(solution)/shard_map/all_gather | solution.py:85
  63.7 7.3 %collective-permute-start.2 = (bf16[30,256]{1,0:T(8,128)(2,1)S(1)}, bf16[30,256]{1,0:T(8,128)(2,1)S(1)}, u32[]{:S(2)}, u32[]{:S(2)}) collective-permute-start(bf16[30,256]{1,0:T(8,128)(2,1)S(1)} %get-tuple-element.36), channel_id=1, source_target_pairs={{0,1},{1,2},{2,3},{3,4},{4,5},{5,6},{6,7},{8,9},{9,10},{10,11},{11... | collective-permute-start | bytes 46088 | tf_op jit(solution)/shard_map/ppermute | solution.py:19
  68.6 7.3 %collective-permute-start.3 = (bf16[30,256]{1,0:T(8,128)(2,1)S(1)}, bf16[30,256]{1,0:T(8,128)(2,1)S(1)}, u32[]{:S(2)}, u32[]{:S(2)}) collective-permute-start(bf16[30,256]{1,0:T(8,128)(2,1)S(1)} %get-tuple-element.37), channel_id=1, source_target_pairs={{1,0},{2,1},{3,2},{4,3},{5,4},{6,5},{7,6},{9,8},{10,9},{11,10},{12... | collective-permute-start | bytes 46088 | tf_op jit(solution)/shard_map/ppermute | solution.py:21
  71.0 6.8 %collective-permute-start = (bf16[30,256]{1,0:T(8,128)(2,1)S(1)}, bf16[30,256]{1,0:T(8,128)(2,1)S(1)}, u32[]{:S(2)}, u32[]{:S(2)}) collective-permute-start(bf16[30,256]{1,0:T(8,128)(2,1)S(1)} %get-tuple-element.38), channel_id=1, source_target_pairs={{0,1},{1,2},{2,3},{3,4},{4,5},{5,6},{6,7},{8,9},{9,10},{10,11},{11... | collective-permute-start | bytes 46088 | tf_op jit(solution)/shard_map/ppermute | solution.py:19
  75.8 7.0 %collective-permute-start.1 = (bf16[30,256]{1,0:T(8,128)(2,1)S(1)}, bf16[30,256]{1,0:T(8,128)(2,1)S(1)}, u32[]{:S(2)}, u32[]{:S(2)}) collective-permute-start(bf16[30,256]{1,0:T(8,128)(2,1)S(1)} %get-tuple-element.39), channel_id=1, source_target_pairs={{1,0},{2,1},{3,2},{4,3},{5,4},{6,5},{7,6},{9,8},{10,9},{11,10},{12... | collective-permute-start | bytes 46088 | tf_op jit(solution)/shard_map/ppermute | solution.py:21
  77.9 23.7 %collective-permute-start.8 = (bf16[512,128]{1,0:T(8,128)(2,1)}, bf16[512,128]{1,0:T(8,128)(2,1)}, u32[]{:S(2)}, u32[]{:S(2)}) collective-permute-start(bf16[512,128]{1,0:T(8,128)(2,1)} %bitcast.50), channel_id=1, source_target_pairs={{0,1},{1,2},{2,3},{3,4},{4,5},{5,6},{6,7},{8,9},{9,10},{10,11},{11... | collective-permute-start | bytes 393224 | tf_op jit(solution)/shard_map/ppermute | solution.py:31
  91.0 21.4 %copy-start.20 = (bf16[512,128]{0,1:T(8,128)(2,1)}, bf16[512,128]{0,1:T(8,128)(2,1)S(1)}, u32[]{:S(2)}) copy-start(bf16[512,128]{0,1:T(8,128)(2,1)S(1)} %copy.124) | copy-start | bytes 393220
  91.0 24.7 %collective-permute-start.7 = (bf16[512,128]{1,0:T(8,128)(2,1)}, bf16[512,128]{1,0:T(8,128)(2,1)}, u32[]{:S(2)}, u32[]{:S(2)}) collective-permute-start(bf16[512,128]{1,0:T(8,128)(2,1)} %collective-permute-done.6), channel_id=1, source_target_pairs={{1,0},{2,1},{3,2},{4,3},{5,4},{6,5},{7,6},{9,8},{10,9},{11,10},{12... | collective-permute-start | bytes 393224 | tf_op jit(solution)/shard_map/ppermute | solution.py:31
  94.6 15.2 %copy-start.22 = (bf16[512,128]{0,1:T(8,128)(2,1)S(1)}, bf16[512,128]{0,1:T(8,128)(2,1)}, u32[]{:S(2)}) copy-start(bf16[512,128]{0,1:T(8,128)(2,1)} %copy.123) | copy-start | bytes 393220
  94.6 15.2 %copy-start.27 = (pred[512,512]{0,1:T(8,128)(4,1)S(1)}, pred[512,512]{0,1:T(8,128)(4,1)}, u32[]{:S(2)}) copy-start(pred[512,512]{0,1:T(8,128)(4,1)} %get-tuple-element.77) | copy-start | bytes 786436
  94.6 22.1 %collective-permute-start.5 = (bf16[512,128]{1,0:T(8,128)(2,1)}, bf16[512,128]{1,0:T(8,128)(2,1)}, u32[]{:S(2)}, u32[]{:S(2)}) collective-permute-start(bf16[512,128]{1,0:T(8,128)(2,1)} %collective-permute-done.4), channel_id=1, source_target_pairs={{0,1},{1,2},{2,3},{3,4},{4,5},{5,6},{6,7},{8,9},{9,10},{10,11},{11... | collective-permute-start | bytes 393224 | tf_op jit(solution)/shard_map/ppermute | solution.py:31
  99.6 18.9 %collective-permute-start.11 = (bf16[512,128]{1,0:T(8,128)(2,1)}, bf16[512,128]{1,0:T(8,128)(2,1)}, u32[]{:S(2)}, u32[]{:S(2)}) collective-permute-start(bf16[512,128]{1,0:T(8,128)(2,1)} %collective-permute-done.10), channel_id=1, source_target_pairs={{1,0},{2,1},{3,2},{4,3},{5,4},{6,5},{7,6},{9,8},{10,9},{11,10},{12... | collective-permute-start | bytes 393224 | tf_op jit(solution)/shard_map/ppermute | solution.py:31
  101.5 18.6 %collective-permute-start.9 = (bf16[512,128]{1,0:T(8,128)(2,1)}, bf16[512,128]{1,0:T(8,128)(2,1)}, u32[]{:S(2)}, u32[]{:S(2)}) collective-permute-start(bf16[512,128]{1,0:T(8,128)(2,1)} %collective-permute-done.8), channel_id=1, source_target_pairs={{0,1},{1,2},{2,3},{3,4},{4,5},{5,6},{6,7},{8,9},{9,10},{10,11},{11... | collective-permute-start | bytes 393224 | tf_op jit(solution)/shard_map/ppermute | solution.py:31
  116.7 10.1 %copy-start.10 = (bf16[512,128]{0,1:T(8,128)(2,1)}, bf16[512,128]{0,1:T(8,128)(2,1)S(1)}, u32[]{:S(2)}) copy-start(bf16[512,128]{0,1:T(8,128)(2,1)S(1)} %copy.125) | copy-start | bytes 393220
  121.8 3.0 %copy-start.26 = (pred[512,512]{0,1:T(8,128)(4,1)S(1)}, pred[512,512]{0,1:T(8,128)(4,1)}, u32[]{:S(2)}) copy-start(pred[512,512]{0,1:T(8,128)(4,1)} %get-tuple-element.79) | copy-start | bytes 786436
  121.8 5.1 %copy-start.32 = (f32[2,512]{1,0:T(2,128)S(1)}, f32[2,512]{1,0:T(2,128)}, u32[]{:S(2)}) copy-start(f32[2,512]{1,0:T(2,128)} %get-tuple-element.88) | copy-start | bytes 12292
  121.8 5.1 %copy-start.33 = (f32[2,512]{1,0:T(2,128)S(1)}, f32[2,512]{1,0:T(2,128)}, u32[]{:S(2)}) copy-start(f32[2,512]{1,0:T(2,128)} %get-tuple-element.90) | copy-start | bytes 12292
  126.9 8.8 %copy-start.30 = (f32[2,512]{1,0:T(2,128)}, f32[2,512]{1,0:T(2,128)S(1)}, u32[]{:S(2)}) copy-start(f32[2,512]{1,0:T(2,128)S(1)} %get-tuple-element.35) | copy-start | bytes 12292
  140.7 5.4 %copy-start.21 = (bf16[512,128]{0,1:T(8,128)(2,1)S(1)}, bf16[512,128]{0,1:T(8,128)(2,1)}, u32[]{:S(2)}) copy-start(bf16[512,128]{0,1:T(8,128)(2,1)} %copy-done.20) | copy-start | bytes 393220
  145.0 3.1 %copy-start.16 = (bf16[2,64,512]{2,1,0:T(8,128)(2,1)S(1)}, bf16[2,64,512]{2,1,0:T(8,128)(2,1)}, u32[]{:S(2)}) copy-start(bf16[2,64,512]{2,1,0:T(8,128)(2,1)} %convolution_convert_fusion.1) | copy-start | bytes 393220
  145.0 3.8 %copy-start.15 = (bf16[2,64,512]{2,1,0:T(8,128)(2,1)S(1)}, bf16[2,64,512]{2,1,0:T(8,128)(2,1)}, u32[]{:S(2)}) copy-start(bf16[2,64,512]{2,1,0:T(8,128)(2,1)} %convolution_convert_fusion.2) | copy-start | bytes 393220
  145.0 5.4 %copy-start.6 = (bf16[2,512,512]{1,2,0:T(8,128)(2,1)S(1)}, bf16[2,512,512]{1,2,0:T(8,128)(2,1)}, u32[]{:S(2)}) copy-start(bf16[2,512,512]{1,2,0:T(8,128)(2,1)} %get-tuple-element.71) | copy-start | bytes 3145732
  151.5 11.4 %copy-start.5 = (bf16[2,512,512]{1,2,0:T(8,128)(2,1)S(1)}, bf16[2,512,512]{1,2,0:T(8,128)(2,1)}, u32[]{:S(2)}) copy-start(bf16[2,512,512]{1,2,0:T(8,128)(2,1)} %get-tuple-element.75) | copy-start | bytes 3145732
  162.8 3.0 %copy-start.7 = (bf16[2,512,512]{1,2,0:T(8,128)(2,1)S(1)}, bf16[2,512,512]{1,2,0:T(8,128)(2,1)}, u32[]{:S(2)}) copy-start(bf16[2,512,512]{1,2,0:T(8,128)(2,1)} %get-tuple-element.73) | copy-start | bytes 3145732
  162.8 3.0 %copy-start.9 = (f32[2,512,64]{1,2,0:T(8,128)S(1)}, f32[2,512,64]{1,2,0:T(8,128)}, u32[]{:S(2)}) copy-start(f32[2,512,64]{1,2,0:T(8,128)} %fusion.118) | copy-start | bytes 786436
  162.8 3.0 %copy-start.23 = (bf16[512,128]{0,1:T(8,128)(2,1)S(1)}, bf16[512,128]{0,1:T(8,128)(2,1)}, u32[]{:S(2)}) copy-start(bf16[512,128]{0,1:T(8,128)(2,1)} %copy.123) | copy-start | bytes 393220
  168.7 14.6 %collective-permute-start.14 = (bf16[512,128]{1,0:T(8,128)(2,1)}, bf16[512,128]{1,0:T(8,128)(2,1)S(1)}, u32[]{:S(2)}, u32[]{:S(2)}) collective-permute-start(bf16[512,128]{1,0:T(8,128)(2,1)} %copy.145), channel_id=1, source_target_pairs={{0,1},{1,2},{2,3},{3,4},{4,5},{5,6},{6,7},{8,9},{9,10},{10,11},{11... | collective-permute-start | bytes 393224 | tf_op jit(solution)/shard_map/ppermute | solution.py:31
  170.8 14.6 %collective-permute-start.13 = (bf16[512,128]{1,0:T(8,128)(2,1)}, bf16[512,128]{1,0:T(8,128)(2,1)S(1)}, u32[]{:S(2)}, u32[]{:S(2)}) collective-permute-start(bf16[512,128]{1,0:T(8,128)(2,1)} %copy.143), channel_id=1, source_target_pairs={{1,0},{2,1},{3,2},{4,3},{5,4},{6,5},{7,6},{9,8},{10,9},{11,10},{12... | collective-permute-start | bytes 393224 | tf_op jit(solution)/shard_map/ppermute | solution.py:31
  174.6 15.6 %collective-permute-start.12 = (bf16[512,128]{1,0:T(8,128)(2,1)}, bf16[512,128]{1,0:T(8,128)(2,1)S(1)}, u32[]{:S(2)}, u32[]{:S(2)}) collective-permute-start(bf16[512,128]{1,0:T(8,128)(2,1)} %copy.140), channel_id=1, source_target_pairs={{2,0},{3,1},{4,2},{5,3},{6,4},{7,5},{10,8},{11,9},{12,10},{13,11},... | collective-permute-start | bytes 393224 | tf_op jit(solution)/shard_map/ppermute | solution.py:31
  177.0 16.7 %collective-permute-start.15 = (bf16[512,128]{1,0:T(8,128)(2,1)}, bf16[512,128]{1,0:T(8,128)(2,1)S(1)}, u32[]{:S(2)}, u32[]{:S(2)}) collective-permute-start(bf16[512,128]{1,0:T(8,128)(2,1)} %copy.147), channel_id=1, source_target_pairs={{0,2},{1,3},{2,4},{3,5},{4,6},{5,7},{8,10},{9,11},{10,12},{11,13},... | collective-permute-start | bytes 393224 | tf_op jit(solution)/shard_map/ppermute | solution.py:31
  181.0 13.4 %collective-permute-start.16 = (bf16[512,128]{1,0:T(8,128)(2,1)}, bf16[512,128]{1,0:T(8,128)(2,1)S(1)}, u32[]{:S(2)}, u32[]{:S(2)}) collective-permute-start(bf16[512,128]{1,0:T(8,128)(2,1)} %copy.150), channel_id=1, source_target_pairs={{2,0},{3,1},{4,2},{5,3},{6,4},{7,5},{10,8},{11,9},{12,10},{13,11},... | collective-permute-start | bytes 393224 | tf_op jit(solution)/shard_map/ppermute | solution.py:31
  183.4 11.0 %collective-permute-start.17 = (bf16[512,128]{1,0:T(8,128)(2,1)}, bf16[512,128]{1,0:T(8,128)(2,1)S(1)}, u32[]{:S(2)}, u32[]{:S(2)}) collective-permute-start(bf16[512,128]{1,0:T(8,128)(2,1)} %copy.153), channel_id=1, source_target_pairs={{1,0},{2,1},{3,2},{4,3},{5,4},{6,5},{7,6},{9,8},{10,9},{11,10},{12... | collective-permute-start | bytes 393224 | tf_op jit(solution)/shard_map/ppermute | solution.py:31
  185.3 9.1 %collective-permute-start.18 = (bf16[512,128]{1,0:T(8,128)(2,1)}, bf16[512,128]{1,0:T(8,128)(2,1)S(1)}, u32[]{:S(2)}, u32[]{:S(2)}) collective-permute-start(bf16[512,128]{1,0:T(8,128)(2,1)} %copy.155), channel_id=1, source_target_pairs={{0,1},{1,2},{2,3},{3,4},{4,5},{5,6},{6,7},{8,9},{9,10},{10,11},{11... | collective-permute-start | bytes 393224 | tf_op jit(solution)/shard_map/ppermute | solution.py:31
  190.2 7.1 %collective-permute-start.19 = (bf16[512,128]{1,0:T(8,128)(2,1)}, bf16[512,128]{1,0:T(8,128)(2,1)S(1)}, u32[]{:S(2)}, u32[]{:S(2)}) collective-permute-start(bf16[512,128]{1,0:T(8,128)(2,1)} %copy.157), channel_id=1, source_target_pairs={{0,2},{1,3},{2,4},{3,5},{4,6},{5,7},{8,10},{9,11},{10,12},{11,13},... | collective-permute-start | bytes 393224 | tf_op jit(solution)/shard_map/ppermute | solution.py:31
  (12 other events, 21.5 us)
Sparse Core Ops, SparseCore 0:
  88.3 15.9 all-gather.1
where the time goes:
time: 207 us; the launch traced here: 205 us
  starting transfers between devices  84.1 us (41%)
  local copies, waits for them, and re-layouts  39.1 us (19%)
  matrix products  34.8 us (17%)
  other arithmetic  26.7 us (13%)
  between operations  14.9 us (7%)
  waiting for transfers between devices  5.17 us (2%)
    ppermute x16, starting transfers between devices, shifted(): lax.ppermute(value, axis, [(source, source + steps) for source in range(f...  51.5 us
    unnamed x90, local copies, waits for them, and re-layouts  13.2 us
    dot_general x5, matrix products, block_logits(): jnp.einsum('qhd,khd->hqk', query_heads, keys_now, preferred_element_type=...  12.6 us
    ppermute x8, local copies, waits for them, and re-layouts, shifted(): lax.ppermute(value, axis, [(source, source + steps) for source in range(f...  12 us
    ppermute x2, starting transfers between devices, padded(): lax.ppermute(tail, axis, [(i, (i + 1) % count) for i in range(ends)])  9.64 us
    unnamed x5, other arithmetic  8.65 us
    dot_general x5, matrix products, on_device(): jnp.einsum('hqk,qhd->khd', dlogits, query_heads, preferred_element_type=j...  7.3 us
    reshape x4, local copies, waits for them, and re-layouts, on_device(): key_part = (jnp.einsum('hqk,qhd->khd', dlogits, query_heads, preferred_el...  6.71 us
  transfers between devices with their start and end apart: 26, of which 2 were waited for; matrix products, arithmetic and copies ran while one was open for 27% of the time, Pallas kernels for 0%

commit v1 on v0

--- a/solution.py
+++ b/solution.py
@@ -58,7 +58,12 @@
     moved = (
         lax.all_to_all(query, "head", split_axis=2, concat_axis=1, tiled=True),
         lax.all_to_all(key, "head", split_axis=2, concat_axis=1, tiled=True),
-        lax.all_to_all(value, "head", split_axis=2, concat_axis=1, tiled=True),
+        jnp.concatenate(
+            lax.all_to_all(
+                jnp.stack(jnp.split(value, lax.axis_size("head"), axis=2)), "head", 0, 0
+            ),
+            axis=1,
+        ),
         lax.all_to_all(resid_in, "head", split_axis=2, concat_axis=1, tiled=True),
         lax.all_to_all(out_grad, "head", split_axis=2, concat_axis=1, tiled=True),
     )

time: 207 us -> 200 us (0.966)
  local copies, waits for them, and re-layouts: 39.1 us -> 30 us
  matrix products: 34.8 us -> 38.3 us
    ppermute x8 -> x4, local copies, waits for them, and re-layouts: 12 us -> 5.4 us  [shifted(): lax.ppermute(value, axis, [(source, source + steps) for source in range(f...]
    unnamed x90 -> x72, local copies, waits for them, and re-layouts: 13.2 us -> 8.2 us
    dot_general x5, matrix products: 3 us -> 7.08 us  [block_slopes(): jnp.einsum('qhd,khd->hqk', grad_heads, values_now, preferred_element_type...]
    all_to_all x1, waiting for transfers between devices: 0.01 us -> 2.25 us  [on_device(): lax.all_to_all(query, 'head', split_axis=2, concat_axis=1, tiled=True)]
    all_to_all x1, waiting for transfers between devices: 2.25 us -> 0.01 us  [on_device(): lax.all_to_all(key, 'head', split_axis=2, concat_axis=1, tiled=True)]
    unnamed x5 -> x4, other arithmetic: 8.65 us -> 7.24 us
  transfers between devices with their start and end apart: 26 -> 26, of which waited for: 2 -> 2; matrix products, arithmetic and copies ran while one was open for 27% -> 28% of each run, Pallas kernels for 0% -> 0%
where the time goes in v1:
time: 200 us; the launch traced here: 198 us
  starting transfers between devices  84 us (42%)
  matrix products  38.3 us (19%)
  local copies, waits for them, and re-layouts  30 us (15%)
  other arithmetic  26 us (13%)
  between operations  14.9 us (7%)
  waiting for transfers between devices  5.18 us (3%)
    ppermute x16, starting transfers between devices, shifted(): lax.ppermute(value, axis, [(source, source + steps) for source in range(f...  51.5 us
    dot_general x5, matrix products, block_logits(): jnp.einsum('qhd,khd->hqk', query_heads, keys_now, preferred_element_type=...  11.4 us
    ppermute x2, starting transfers between devices, padded(): lax.ppermute(tail, axis, [(i, (i + 1) % count) for i in range(ends)])  9.64 us
    unnamed x72, local copies, waits for them, and re-layouts  8.2 us
    dot_general x5, matrix products, on_device(): jnp.einsum('hqk,qhd->khd', dlogits, query_heads, preferred_element_type=j...  7.27 us
    unnamed x4, other arithmetic  7.24 us
    dot_general x5, matrix products, block_slopes(): jnp.einsum('qhd,khd->hqk', grad_heads, values_now, preferred_element_type...  7.08 us
    reshape x4, local copies, waits for them, and re-layouts, on_device(): key_part = (jnp.einsum('hqk,qhd->khd', dlogits, query_heads, preferred_el...  6.73 us
  transfers between devices with their start and end apart: 26, of which 2 were waited for; matrix products, arithmetic and copies ran while one was open for 28% of the time, Pallas kernels for 0%

profile of v1, /device:TPU:14, one launch (start us, length us, event | category | flops | bytes accessed | tf_op | source)
XLA Modules:
  0.0 198.4 jit_solution(15439866209692085374)
XLA Ops:
  8.8 3.8 %all-to-all-start.4 = ((bf16[4,1,128,128]{3,2,1,0:T(8,128)(2,1)}), bf16[4,1,128,128]{3,2,1,0:T(8,128)(2,1)S(1)}, u32[]{:S(2)}, u32[]{:S(2)}) async-start(bf16[4,1,128,128]{3,2,1,0:T(8,128)(2,1)} %pad_maximum_fusion), calls=%async_computation.4 | async-start | bytes 262144 | tf_op jit(solution)/shard_map/all_to_all | solution.py:62
  17.5 2.9 %fusion.33 = (pred[512,512]{0,1:T(8,128)(4,1)}, pred[512,512]{0,1:T(8,128)(4,1)}, pred[512,512]{0,1:T(8,128)(4,1)}, pred[512,512]{0,1:T(8,128)(4,1)}, pred[512,512]{0,1:T(8,128)(4,1)}) fusion(s32[512]{0:T(512)S(1)} %get-tuple-element.112, s32[512]{0:T(512)S(1)} %iota_add_fusion.4, pred[512]{0:T(512)(128)(4,1)S(1)} %get-tuple-element.110, pred[]{:T(512)S(6)} %and.169, ...), kind=kLoop, calls=%fused_computation.72 | loop fusion | flops 6553600 | bytes 1323525 | tf_op jit(solution)/shard_map/and | solution.py:115
  25.6 3.4 %all-to-all-start.2 = ((bf16[4,2,8192]{2,1,0:T(2,128)(2,1)}), bf16[4,2,8192]{2,1,0:T(2,128)(2,1)S(1)}, u32[]{:S(2)}, u32[]{:S(2)}) async-start(bf16[4,2,8192]{2,1,0:T(2,128)(2,1)} %reshape.503), calls=%async_computation.2 | async-start | bytes 262144 | tf_op jit(solution)/shard_map/all_to_all | solution.py:59
  29.7 2.2 %all-to-all-done.2 = bf16[4,2,8192]{2,1,0:T(2,128)(2,1)S(1)} async-done(((bf16[4,2,8192]{2,1,0:T(2,128)(2,1)}), bf16[4,2,8192]{2,1,0:T(2,128)(2,1)S(1)}, u32[]{:S(2)}, u32[]{:S(2)}) %all-to-all-start.2) | async-done | bytes 131104 | tf_op jit(solution)/shard_map/all_to_all | solution.py:59
  31.9 5.0 %all-to-all-start.3 = ((bf16[4,2,8192]{2,1,0:T(2,128)(2,1)}), bf16[4,2,8192]{2,1,0:T(2,128)(2,1)S(1)}, u32[]{:S(2)}, u32[]{:S(2)}) async-start(bf16[4,2,8192]{2,1,0:T(2,128)(2,1)} %reshape.501), calls=%async_computation.3 | async-start | bytes 262144 | tf_op jit(solution)/shard_map/all_to_all | solution.py:60
  37.3 2.2 %reduce.1 = bf16[1024,128]{1,0:T(8,128)(2,1)S(1)} reduce(bf16[1024,1,128]{2,1,0:T(2,128)(2,1)S(1)} %bitcast.180, bf16[]{:T(256)} %broadcast.279), dimensions={1}, to_apply=%bitcast.115.reduce_sub_computation | reduce | bytes 524290
  40.7 2.2 %reduce = bf16[1024,128]{1,0:T(8,128)(2,1)S(1)} reduce(bf16[1024,1,128]{2,1,0:T(2,128)(2,1)S(1)} %bitcast.179, bf16[]{:T(256)} %broadcast.279), dimensions={1}, to_apply=%bitcast.113.reduce_sub_computation | reduce | bytes 524290
  43.7 3.4 %all-to-all-start.1 = ((bf16[4,2,16384]{2,1,0:T(2,128)(2,1)}), bf16[4,2,16384]{2,1,0:T(2,128)(2,1)S(1)}, u32[]{:S(2)}, u32[]{:S(2)}) async-start(bf16[4,2,16384]{2,1,0:T(2,128)(2,1)} %reshape.499), calls=%async_computation.1 | async-start | bytes 524288 | tf_op jit(solution)/shard_map/all_to_all | solution.py:67
  47.9 2.4 %collective-permute-start.10 = (bf16[512,128]{0,1:T(8,128)(2,1)}, bf16[512,128]{0,1:T(8,128)(2,1)}, u32[]{:S(2)}, u32[]{:S(2)}) collective-permute-start(bf16[512,128]{0,1:T(8,128)(2,1)} %copy.131), channel_id=1, source_target_pairs={{1,0},{2,1},{3,2},{4,3},{5,4},{6,5},{7,6},{9,8},{10,9},{11,10},{12... | collective-permute-start | bytes 393224 | tf_op jit(solution)/shard_map/ppermute | solution.py:31
  50.3 4.3 %collective-permute-start.8 = (bf16[512,128]{0,1:T(8,128)(2,1)}, bf16[512,128]{0,1:T(8,128)(2,1)}, u32[]{:S(2)}, u32[]{:S(2)}) collective-permute-start(bf16[512,128]{0,1:T(8,128)(2,1)} %copy.131), channel_id=1, source_target_pairs={{0,1},{1,2},{2,3},{3,4},{4,5},{5,6},{6,7},{8,9},{9,10},{10,11},{11... | collective-permute-start | bytes 393224 | tf_op jit(solution)/shard_map/ppermute | solution.py:31
  56.1 1.9 collective-permute-start.6
  58.0 3.4 %all-to-all-start = ((bf16[4,2,16384]{2,1,0:T(2,128)(2,1)}), bf16[4,2,16384]{2,1,0:T(2,128)(2,1)S(1)}, u32[]{:S(2)}, u32[]{:S(2)}) async-start(bf16[4,2,16384]{2,1,0:T(2,128)(2,1)} %reshape.497), calls=%async_computation | async-start | bytes 524288 | tf_op jit(solution)/shard_map/all_to_all | solution.py:68
  62.0 4.8 %collective-permute-start.2 = (bf16[30,256]{1,0:T(8,128)(2,1)S(1)}, bf16[30,256]{1,0:T(8,128)(2,1)S(1)}, u32[]{:S(2)}, u32[]{:S(2)}) collective-permute-start(bf16[30,256]{1,0:T(8,128)(2,1)S(1)} %get-tuple-element.36), channel_id=1, source_target_pairs={{0,1},{1,2},{2,3},{3,4},{4,5},{5,6},{6,7},{8,9},{9,10},{10,11},{11... | collective-permute-start | bytes 46088 | tf_op jit(solution)/shard_map/ppermute | solution.py:19
  66.8 1.9 collective-permute-start.3
  69.3 4.8 %collective-permute-start = (bf16[30,256]{1,0:T(8,128)(2,1)S(1)}, bf16[30,256]{1,0:T(8,128)(2,1)S(1)}, u32[]{:S(2)}, u32[]{:S(2)}) collective-permute-start(bf16[30,256]{1,0:T(8,128)(2,1)S(1)} %get-tuple-element.38), channel_id=1, source_target_pairs={{0,1},{1,2},{2,3},{3,4},{4,5},{5,6},{6,7},{8,9},{9,10},{10,11},{11... | collective-permute-start | bytes 46088 | tf_op jit(solution)/shard_map/ppermute | solution.py:19
  74.1 1.9 collective-permute-start.1
  76.1 5.0 %collective-permute-start.4 = (bf16[512,128]{1,0:T(8,128)(2,1)}, bf16[512,128]{1,0:T(8,128)(2,1)}, u32[]{:S(2)}, u32[]{:S(2)}) collective-permute-start(bf16[512,128]{1,0:T(8,128)(2,1)} %bitcast.40), channel_id=1, source_target_pairs={{0,1},{1,2},{2,3},{3,4},{4,5},{5,6},{6,7},{8,9},{9,10},{10,11},{11... | collective-permute-start | bytes 393224 | tf_op jit(solution)/shard_map/ppermute | solution.py:31
  81.2 2.4 %slice_multiply_fusion.31 = f32[542,256]{1,0:T(8,128)S(1)} fusion(f32[572,256]{1,0:T(8,128)S(1)} %maximum_convert_fusion, f32[572,256]{1,0:T(8,128)S(1)} %maximum_convert_fusion.1, f32[256]{0:T(256)S(1)} %bitcast.217, f32[256]{0:T(256)S(1)} %bitcast.219, f32[256]{0:T(256)S(1)} %bitcast.221, f32[256]{0:T(256)S(1)} %bitcast.223, f32[256]{0:T(256)S(1)} %bitcast.225, ...), kind=kLoop, calls=%fused_computation.140 | loop fusion | flops 9573888 | bytes 18347008 | tf_op jit(solution)/shard_map/mul | solution.py:46
  83.6 2.8 %fusion.71 = bf16[512,256]{1,0:T(8,128)(2,1)} fusion(f32[542,256]{1,0:T(8,128)S(1)} %slice_multiply_fusion.31, f32[572,256]{1,0:T(8,128)S(1)} %maximum_convert_fusion, f32[256]{0:T(256)S(1)} %bitcast.218, f32[256]{0:T(256)S(1)} %bitcast.220, f32[256]{0:T(256)S(1)} %bitcast.222, f32[256]{0:T(256)S(1)} %bitcast.224, f32[256]{0:T(256)S(1)} %bitcast.226, ...), kind=kLoop, calls=%fused_computation.143 | loop fusion | flops 8257536 | bytes 17071104 | tf_op jit(solution)/shard_map/convert_element_type | solution.py:51
  90.8 1.9 collective-permute-start.7
  92.8 1.7 copy.127
  94.5 4.9 %collective-permute-start.5 = (bf16[512,128]{1,0:T(8,128)(2,1)}, bf16[512,128]{1,0:T(8,128)(2,1)}, u32[]{:S(2)}, u32[]{:S(2)}) collective-permute-start(bf16[512,128]{1,0:T(8,128)(2,1)} %collective-permute-done.4), channel_id=1, source_target_pairs={{0,1},{1,2},{2,3},{3,4},{4,5},{5,6},{6,7},{8,9},{9,10},{10,11},{11... | collective-permute-start | bytes 393224 | tf_op jit(solution)/shard_map/ppermute | solution.py:31
  99.4 2.9 %fusion.113 = (f32[2,512]{1,0:T(2,128)S(1)}, f32[2,512,512]{1,2,0:T(8,128)}) fusion(bf16[512,2,64]{0,2,1:T(8,128)(2,1)S(1)} %reshape_squeeze.8, bf16[512,2,64]{0,2,1:T(8,128)(2,1)S(1)} %bitcast.209, pred[512,512]{0,1:T(8,128)(4,1)} %get-tuple-element.82), kind=kOutput, calls=%fused_computation.242 | convolution fusion | flops 68680704 | bytes 2625536 | tf_op jit(solution)/shard_map/qhd,khd->hqk/dot_general | solution.py:130
  102.3 1.9 fusion.114
  104.2 1.9 collective-permute-start.11
  106.2 4.8 %collective-permute-start.9 = (bf16[512,128]{0,1:T(8,128)(2,1)}, bf16[512,128]{0,1:T(8,128)(2,1)}, u32[]{:S(2)}, u32[]{:S(2)}) collective-permute-start(bf16[512,128]{0,1:T(8,128)(2,1)} %collective-permute-done.8), channel_id=1, source_target_pairs={{0,1},{1,2},{2,3},{3,4},{4,5},{5,6},{6,7},{8,9},{9,10},{10,11},{11... | collective-permute-start | bytes 393224 | tf_op jit(solution)/shard_map/ppermute | solution.py:31
  112.0 1.7 copy.126
  113.7 3.0 %fusion.116 = (f32[2,512]{1,0:T(2,128)S(1)}, f32[2,512,512]{1,2,0:T(8,128)}) fusion(bf16[512,2,64]{0,2,1:T(8,128)(2,1)S(1)} %reshape_squeeze.8, bf16[512,2,64]{0,2,1:T(8,128)(2,1)} %bitcast.211, pred[512,512]{0,1:T(8,128)(4,1)} %get-tuple-element.80), kind=kOutput, calls=%fused_computation.245 | convolution fusion | flops 68680704 | bytes 2625536 | tf_op jit(solution)/shard_map/qhd,khd->hqk/dot_general | solution.py:130
  116.8 2.0 %fusion.112 = (f32[2,512]{1,0:T(2,128)S(1)}, f32[2,512,512]{1,2,0:T(8,128)}) fusion(bf16[512,2,64]{0,2,1:T(8,128)(2,1)S(1)} %reshape_squeeze.8, bf16[512,2,64]{0,2,1:T(8,128)(2,1)S(1)} %bitcast.197, pred[512,512]{0,1:T(8,128)(4,1)S(1)} %copy-done.23), kind=kOutput, calls=%fused_computation.241 | convolution fusion | flops 68680704 | bytes 2625536 | tf_op jit(solution)/shard_map/qhd,khd->hqk/dot_general | solution.py:130
  118.8 1.7 convolution_convert_fusion.5
  122.2 1.7 multiply_reduce_fusion
  134.4 4.2 %multiply_convert_fusion = (bf16[2,512,512]{1,2,0:T(8,128)(2,1)}, bf16[2,512,512]{1,2,0:T(8,128)(2,1)}, bf16[2,512,512]{1,2,0:T(8,128)(2,1)}, bf16[2,512,512]{1,2,0:T(8,128)(2,1)S(1)}, bf16[2,512,512]{1,2,0:T(8,128)(2,1)}) fusion(f32[2,512,512]{1,2,0:T(8,128)S(1)} %get-tuple-element.100, f32[2,512,512]{1,2,0:T(8,128)S(1)} %copy-done.4, ...), kind=kLoop, calls=%fused_computation | loop fusion | flops 10485760 | bytes 26222592 | tf_op jit(solution)/shard_map/convert_element_type | solution.py:164
  145.0 1.7 copy.147
  146.8 2.3 %fusion.15 = bf16[2,512,64]{1,2,0:T(8,128)(2,1)} fusion(bf16[2,512,512]{1,2,0:T(8,128)(2,1)} %get-tuple-element.76, bf16[512,2,64]{0,2,1:T(8,128)(2,1)S(1)} %reshape_squeeze.8), kind=kOutput, calls=%fused_computation.54 | convolution fusion | flops 67239936 | bytes 1310720 | tf_op jit(solution)/shard_map/hqk,qhd->khd/dot_general | solution.py:173
  149.1 1.7 copy.140
  150.8 2.3 %fusion.16 = bf16[2,512,64]{1,2,0:T(8,128)(2,1)} fusion(bf16[2,512,512]{1,2,0:T(8,128)(2,1)} %get-tuple-element.77, bf16[512,2,64]{0,2,1:T(8,128)(2,1)S(1)} %reshape_squeeze.8), kind=kOutput, calls=%fused_computation.55 | convolution fusion | flops 67239936 | bytes 1310720 | tf_op jit(solution)/shard_map/hqk,qhd->khd/dot_general | solution.py:173
  153.1 1.7 copy.143
  154.7 1.7 copy.145
  160.7 1.7 copy.158
  162.3 2.0 %collective-permute-start.14 = (bf16[512,128]{1,0:T(8,128)(2,1)}, bf16[512,128]{1,0:T(8,128)(2,1)S(1)}, u32[]{:S(2)}, u32[]{:S(2)}) collective-permute-start(bf16[512,128]{1,0:T(8,128)(2,1)} %copy.145), channel_id=1, source_target_pairs={{0,1},{1,2},{2,3},{3,4},{4,5},{5,6},{6,7},{8,9},{9,10},{10,11},{11... | collective-permute-start | bytes 393224 | tf_op jit(solution)/shard_map/ppermute | solution.py:31
  164.4 3.8 %collective-permute-start.13 = (bf16[512,128]{1,0:T(8,128)(2,1)}, bf16[512,128]{1,0:T(8,128)(2,1)S(1)}, u32[]{:S(2)}, u32[]{:S(2)}) collective-permute-start(bf16[512,128]{1,0:T(8,128)(2,1)} %copy.143), channel_id=1, source_target_pairs={{1,0},{2,1},{3,2},{4,3},{5,4},{6,5},{7,6},{9,8},{10,9},{11,10},{12... | collective-permute-start | bytes 393224 | tf_op jit(solution)/shard_map/ppermute | solution.py:31
  168.2 2.4 %collective-permute-start.12 = (bf16[512,128]{1,0:T(8,128)(2,1)}, bf16[512,128]{1,0:T(8,128)(2,1)S(1)}, u32[]{:S(2)}, u32[]{:S(2)}) collective-permute-start(bf16[512,128]{1,0:T(8,128)(2,1)} %copy.140), channel_id=1, source_target_pairs={{2,0},{3,1},{4,2},{5,3},{6,4},{7,5},{10,8},{11,9},{12,10},{13,11},... | collective-permute-start | bytes 393224 | tf_op jit(solution)/shard_map/ppermute | solution.py:31
  170.6 3.5 %collective-permute-start.15 = (bf16[512,128]{1,0:T(8,128)(2,1)}, bf16[512,128]{1,0:T(8,128)(2,1)S(1)}, u32[]{:S(2)}, u32[]{:S(2)}) collective-permute-start(bf16[512,128]{1,0:T(8,128)(2,1)} %copy.147), channel_id=1, source_target_pairs={{0,2},{1,3},{2,4},{3,5},{4,6},{5,7},{8,10},{9,11},{10,12},{11,13},... | collective-permute-start | bytes 393224 | tf_op jit(solution)/shard_map/ppermute | solution.py:31
  174.6 2.4 %collective-permute-start.16 = (bf16[512,128]{1,0:T(8,128)(2,1)}, bf16[512,128]{1,0:T(8,128)(2,1)S(1)}, u32[]{:S(2)}, u32[]{:S(2)}) collective-permute-start(bf16[512,128]{1,0:T(8,128)(2,1)} %copy.150), channel_id=1, source_target_pairs={{2,0},{3,1},{4,2},{5,3},{6,4},{7,5},{10,8},{11,9},{12,10},{13,11},... | collective-permute-start | bytes 393224 | tf_op jit(solution)/shard_map/ppermute | solution.py:31
  177.0 1.9 collective-permute-start.17
  178.9 4.8 %collective-permute-start.18 = (bf16[512,128]{1,0:T(8,128)(2,1)}, bf16[512,128]{1,0:T(8,128)(2,1)S(1)}, u32[]{:S(2)}, u32[]{:S(2)}) collective-permute-start(bf16[512,128]{1,0:T(8,128)(2,1)} %copy.155), channel_id=1, source_target_pairs={{0,1},{1,2},{2,3},{3,4},{4,5},{5,6},{6,7},{8,9},{9,10},{10,11},{11... | collective-permute-start | bytes 393224 | tf_op jit(solution)/shard_map/ppermute | solution.py:31
  183.8 3.5 %collective-permute-start.19 = (bf16[512,128]{1,0:T(8,128)(2,1)}, bf16[512,128]{1,0:T(8,128)(2,1)S(1)}, u32[]{:S(2)}, u32[]{:S(2)}) collective-permute-start(bf16[512,128]{1,0:T(8,128)(2,1)} %copy.157), channel_id=1, source_target_pairs={{0,2},{1,3},{2,4},{3,5},{4,6},{5,7},{8,10},{9,11},{10,12},{11,13},... | collective-permute-start | bytes 393224 | tf_op jit(solution)/shard_map/ppermute | solution.py:31
  188.0 2.8 %collective-permute-done.19 = bf16[512,128]{1,0:T(8,128)(2,1)S(1)} collective-permute-done((bf16[512,128]{1,0:T(8,128)(2,1)}, bf16[512,128]{1,0:T(8,128)(2,1)S(1)}, u32[]{:S(2)}, u32[]{:S(2)}) %collective-permute-start.19) | collective-permute-done | bytes 131104 | tf_op jit(solution)/shard_map/ppermute | solution.py:31
  (156 shorter events, 47.9 us)
Async XLA Ops:
  7.2 111.7 %copy-start = (bf16[512,1024]{1,0:T(8,128)(2,1)S(1)}, bf16[512,1024]{1,0:T(8,128)(2,1)}, u32[]{:S(2)}) copy-start(bf16[512,1024]{1,0:T(8,128)(2,1)} %param.13) | copy-start | bytes 3145732
  7.2 13.3 %copy-start.25 = (bf16[1,128,512]{2,1,0:T(8,128)(2,1)S(1)}, bf16[1,128,512]{2,1,0:T(8,128)(2,1)}, u32[]{:S(2)}) copy-start(bf16[1,128,512]{2,1,0:T(8,128)(2,1)} %param.8) | copy-start | bytes 393220
  7.2 16.1 %copy-start.26 = (bf16[1,128,512]{2,1,0:T(8,128)(2,1)S(1)}, bf16[1,128,512]{2,1,0:T(8,128)(2,1)}, u32[]{:S(2)}) copy-start(bf16[1,128,512]{2,1,0:T(8,128)(2,1)} %param.9) | copy-start | bytes 393220
  8.8 16.8 %all-to-all-start.4 = ((bf16[4,1,128,128]{3,2,1,0:T(8,128)(2,1)}), bf16[4,1,128,128]{3,2,1,0:T(8,128)(2,1)S(1)}, u32[]{:S(2)}, u32[]{:S(2)}) async-start(bf16[4,1,128,128]{3,2,1,0:T(8,128)(2,1)} %pad_maximum_fusion), calls=%async_computation.4 | async-start | bytes 262144 | tf_op jit(solution)/shard_map/all_to_all | solution.py:62
  12.6 24.3 %copy-start.21 = (bf16[1,128,1024]{2,1,0:T(8,128)(2,1)S(1)}, bf16[1,128,1024]{2,1,0:T(8,128)(2,1)}, u32[]{:S(2)}) copy-start(bf16[1,128,1024]{2,1,0:T(8,128)(2,1)} %param.11) | copy-start | bytes 786436
  22.6 17.7 %copy-start.22 = (bf16[1,128,1024]{2,1,0:T(8,128)(2,1)S(1)}, bf16[1,128,1024]{2,1,0:T(8,128)(2,1)}, u32[]{:S(2)}) copy-start(bf16[1,128,1024]{2,1,0:T(8,128)(2,1)} %param.12) | copy-start | bytes 786436
  25.6 6.4 %all-to-all-start.2 = ((bf16[4,2,8192]{2,1,0:T(2,128)(2,1)}), bf16[4,2,8192]{2,1,0:T(2,128)(2,1)S(1)}, u32[]{:S(2)}, u32[]{:S(2)}) async-start(bf16[4,2,8192]{2,1,0:T(2,128)(2,1)} %reshape.503), calls=%async_computation.2 | async-start | bytes 262144 | tf_op jit(solution)/shard_map/all_to_all | solution.py:59
  31.9 11.8 %all-to-all-start.3 = ((bf16[4,2,8192]{2,1,0:T(2,128)(2,1)}), bf16[4,2,8192]{2,1,0:T(2,128)(2,1)S(1)}, u32[]{:S(2)}, u32[]{:S(2)}) async-start(bf16[4,2,8192]{2,1,0:T(2,128)(2,1)} %reshape.501), calls=%async_computation.3 | async-start | bytes 262144 | tf_op jit(solution)/shard_map/all_to_all | solution.py:60
  43.7 14.3 %all-to-all-start.1 = ((bf16[4,2,16384]{2,1,0:T(2,128)(2,1)}), bf16[4,2,16384]{2,1,0:T(2,128)(2,1)S(1)}, u32[]{:S(2)}, u32[]{:S(2)}) async-start(bf16[4,2,16384]{2,1,0:T(2,128)(2,1)} %reshape.499), calls=%async_computation.1 | async-start | bytes 524288 | tf_op jit(solution)/shard_map/all_to_all | solution.py:67
  47.9 56.3 %collective-permute-start.10 = (bf16[512,128]{0,1:T(8,128)(2,1)}, bf16[512,128]{0,1:T(8,128)(2,1)}, u32[]{:S(2)}, u32[]{:S(2)}) collective-permute-start(bf16[512,128]{0,1:T(8,128)(2,1)} %copy.131), channel_id=1, source_target_pairs={{1,0},{2,1},{3,2},{4,3},{5,4},{6,5},{7,6},{9,8},{10,9},{11,10},{12... | collective-permute-start | bytes 393224 | tf_op jit(solution)/shard_map/ppermute | solution.py:31
  50.3 55.8 %collective-permute-start.8 = (bf16[512,128]{0,1:T(8,128)(2,1)}, bf16[512,128]{0,1:T(8,128)(2,1)}, u32[]{:S(2)}, u32[]{:S(2)}) collective-permute-start(bf16[512,128]{0,1:T(8,128)(2,1)} %copy.131), channel_id=1, source_target_pairs={{0,1},{1,2},{2,3},{3,4},{4,5},{5,6},{6,7},{8,9},{9,10},{10,11},{11... | collective-permute-start | bytes 393224 | tf_op jit(solution)/shard_map/ppermute | solution.py:31
  56.1 30.4 %copy-start.16 = (bf16[512,2,64]{0,2,1:T(8,128)(2,1)}, bf16[512,2,64]{0,2,1:T(8,128)(2,1)S(1)}, u32[]{:S(2)}) copy-start(bf16[512,2,64]{0,2,1:T(8,128)(2,1)S(1)} %reshape_squeeze.9) | copy-start | bytes 393220
  56.1 33.7 %collective-permute-start.6 = (bf16[512,128]{1,0:T(8,128)(2,1)}, bf16[512,128]{1,0:T(8,128)(2,1)}, u32[]{:S(2)}, u32[]{:S(2)}) collective-permute-start(bf16[512,128]{1,0:T(8,128)(2,1)} %bitcast.40), channel_id=1, source_target_pairs={{1,0},{2,1},{3,2},{4,3},{5,4},{6,5},{7,6},{9,8},{10,9},{11,10},{12... | collective-permute-start | bytes 393224 | tf_op jit(solution)/shard_map/ppermute | solution.py:31
  58.0 10.7 %all-to-all-start = ((bf16[4,2,16384]{2,1,0:T(2,128)(2,1)}), bf16[4,2,16384]{2,1,0:T(2,128)(2,1)S(1)}, u32[]{:S(2)}, u32[]{:S(2)}) async-start(bf16[4,2,16384]{2,1,0:T(2,128)(2,1)} %reshape.497), calls=%async_computation | async-start | bytes 524288 | tf_op jit(solution)/shard_map/all_to_all | solution.py:68
  61.4 57.4 %all-gather.2.cloned.1.call-start = ((), (), s32[]{:S(2)}) async-start(), calls=%async_computation.5 | async-start | bytes 1310720 | tf_op jit(solution)/shard_map/all_gather | solution.py:90
  62.0 7.3 %collective-permute-start.2 = (bf16[30,256]{1,0:T(8,128)(2,1)S(1)}, bf16[30,256]{1,0:T(8,128)(2,1)S(1)}, u32[]{:S(2)}, u32[]{:S(2)}) collective-permute-start(bf16[30,256]{1,0:T(8,128)(2,1)S(1)} %get-tuple-element.36), channel_id=1, source_target_pairs={{0,1},{1,2},{2,3},{3,4},{4,5},{5,6},{6,7},{8,9},{9,10},{10,11},{11... | collective-permute-start | bytes 46088 | tf_op jit(solution)/shard_map/ppermute | solution.py:19
  66.8 7.3 %collective-permute-start.3 = (bf16[30,256]{1,0:T(8,128)(2,1)S(1)}, bf16[30,256]{1,0:T(8,128)(2,1)S(1)}, u32[]{:S(2)}, u32[]{:S(2)}) collective-permute-start(bf16[30,256]{1,0:T(8,128)(2,1)S(1)} %get-tuple-element.37), channel_id=1, source_target_pairs={{1,0},{2,1},{3,2},{4,3},{5,4},{6,5},{7,6},{9,8},{10,9},{11,10},{12... | collective-permute-start | bytes 46088 | tf_op jit(solution)/shard_map/ppermute | solution.py:21
  69.3 6.8 %collective-permute-start = (bf16[30,256]{1,0:T(8,128)(2,1)S(1)}, bf16[30,256]{1,0:T(8,128)(2,1)S(1)}, u32[]{:S(2)}, u32[]{:S(2)}) collective-permute-start(bf16[30,256]{1,0:T(8,128)(2,1)S(1)} %get-tuple-element.38), channel_id=1, source_target_pairs={{0,1},{1,2},{2,3},{3,4},{4,5},{5,6},{6,7},{8,9},{9,10},{10,11},{11... | collective-permute-start | bytes 46088 | tf_op jit(solution)/shard_map/ppermute | solution.py:19
  74.1 7.0 %collective-permute-start.1 = (bf16[30,256]{1,0:T(8,128)(2,1)S(1)}, bf16[30,256]{1,0:T(8,128)(2,1)S(1)}, u32[]{:S(2)}, u32[]{:S(2)}) collective-permute-start(bf16[30,256]{1,0:T(8,128)(2,1)S(1)} %get-tuple-element.39), channel_id=1, source_target_pairs={{1,0},{2,1},{3,2},{4,3},{5,4},{6,5},{7,6},{9,8},{10,9},{11,10},{12... | collective-permute-start | bytes 46088 | tf_op jit(solution)/shard_map/ppermute | solution.py:21
  76.1 16.7 %collective-permute-start.4 = (bf16[512,128]{1,0:T(8,128)(2,1)}, bf16[512,128]{1,0:T(8,128)(2,1)}, u32[]{:S(2)}, u32[]{:S(2)}) collective-permute-start(bf16[512,128]{1,0:T(8,128)(2,1)} %bitcast.40), channel_id=1, source_target_pairs={{0,1},{1,2},{2,3},{3,4},{4,5},{5,6},{6,7},{8,9},{9,10},{10,11},{11... | collective-permute-start | bytes 393224 | tf_op jit(solution)/shard_map/ppermute | solution.py:31
  90.8 13.4 %copy-start.17 = (bf16[512,128]{0,1:T(8,128)(2,1)}, bf16[512,128]{0,1:T(8,128)(2,1)S(1)}, u32[]{:S(2)}) copy-start(bf16[512,128]{0,1:T(8,128)(2,1)S(1)} %copy.128) | copy-start | bytes 393220
  90.8 20.1 %collective-permute-start.7 = (bf16[512,128]{1,0:T(8,128)(2,1)}, bf16[512,128]{1,0:T(8,128)(2,1)}, u32[]{:S(2)}, u32[]{:S(2)}) collective-permute-start(bf16[512,128]{1,0:T(8,128)(2,1)} %collective-permute-done.6), channel_id=1, source_target_pairs={{1,0},{2,1},{3,2},{4,3},{5,4},{6,5},{7,6},{9,8},{10,9},{11,10},{12... | collective-permute-start | bytes 393224 | tf_op jit(solution)/shard_map/ppermute | solution.py:31
  94.5 7.8 %copy-start.19 = (bf16[512,128]{0,1:T(8,128)(2,1)S(1)}, bf16[512,128]{0,1:T(8,128)(2,1)}, u32[]{:S(2)}) copy-start(bf16[512,128]{0,1:T(8,128)(2,1)} %copy.127) | copy-start | bytes 393220
  94.5 7.9 %copy-start.24 = (pred[512,512]{0,1:T(8,128)(4,1)S(1)}, pred[512,512]{0,1:T(8,128)(4,1)}, u32[]{:S(2)}) copy-start(pred[512,512]{0,1:T(8,128)(4,1)} %get-tuple-element.81) | copy-start | bytes 786436
  94.5 17.6 %collective-permute-start.5 = (bf16[512,128]{1,0:T(8,128)(2,1)}, bf16[512,128]{1,0:T(8,128)(2,1)}, u32[]{:S(2)}, u32[]{:S(2)}) collective-permute-start(bf16[512,128]{1,0:T(8,128)(2,1)} %collective-permute-done.4), channel_id=1, source_target_pairs={{0,1},{1,2},{2,3},{3,4},{4,5},{5,6},{6,7},{8,9},{9,10},{10,11},{11... | collective-permute-start | bytes 393224 | tf_op jit(solution)/shard_map/ppermute | solution.py:31
  104.2 17.0 %collective-permute-start.11 = (bf16[512,128]{0,1:T(8,128)(2,1)}, bf16[512,128]{0,1:T(8,128)(2,1)}, u32[]{:S(2)}, u32[]{:S(2)}) collective-permute-start(bf16[512,128]{0,1:T(8,128)(2,1)} %collective-permute-done.10), channel_id=1, source_target_pairs={{1,0},{2,1},{3,2},{4,3},{5,4},{6,5},{7,6},{9,8},{10,9},{11,10},{12... | collective-permute-start | bytes 393224 | tf_op jit(solution)/shard_map/ppermute | solution.py:31
  106.2 21.0 %collective-permute-start.9 = (bf16[512,128]{0,1:T(8,128)(2,1)}, bf16[512,128]{0,1:T(8,128)(2,1)}, u32[]{:S(2)}, u32[]{:S(2)}) collective-permute-start(bf16[512,128]{0,1:T(8,128)(2,1)} %collective-permute-done.8), channel_id=1, source_target_pairs={{0,1},{1,2},{2,3},{3,4},{4,5},{5,6},{6,7},{8,9},{9,10},{10,11},{11... | collective-permute-start | bytes 393224 | tf_op jit(solution)/shard_map/ppermute | solution.py:31
  112.0 6.8 %copy-start.10 = (bf16[512,128]{0,1:T(8,128)(2,1)}, bf16[512,128]{0,1:T(8,128)(2,1)S(1)}, u32[]{:S(2)}) copy-start(bf16[512,128]{0,1:T(8,128)(2,1)S(1)} %copy.129) | copy-start | bytes 393220
  113.7 3.0 %copy-start.23 = (pred[512,512]{0,1:T(8,128)(4,1)S(1)}, pred[512,512]{0,1:T(8,128)(4,1)}, u32[]{:S(2)}) copy-start(pred[512,512]{0,1:T(8,128)(4,1)} %get-tuple-element.83) | copy-start | bytes 786436
  134.4 5.4 %copy-start.18 = (bf16[512,128]{0,1:T(8,128)(2,1)S(1)}, bf16[512,128]{0,1:T(8,128)(2,1)}, u32[]{:S(2)}) copy-start(bf16[512,128]{0,1:T(8,128)(2,1)} %copy-done.17) | copy-start | bytes 393220
  138.6 2.1 %copy-start.8 = (f32[2,64,512]{2,1,0:T(8,128)S(1)}, f32[2,64,512]{2,1,0:T(8,128)}, u32[]{:S(2)}) copy-start(f32[2,64,512]{2,1,0:T(8,128)} %fusion.12) | copy-start | bytes 786436
  138.6 2.3 %copy-start.15 = (bf16[2,64,512]{2,1,0:T(8,128)(2,1)S(1)}, bf16[2,64,512]{2,1,0:T(8,128)(2,1)}, u32[]{:S(2)}) copy-start(bf16[2,64,512]{2,1,0:T(8,128)(2,1)} %convolution_convert_fusion) | copy-start | bytes 393220
  138.6 3.0 %copy-start.14 = (bf16[2,64,512]{2,1,0:T(8,128)(2,1)S(1)}, bf16[2,64,512]{2,1,0:T(8,128)(2,1)}, u32[]{:S(2)}) copy-start(bf16[2,64,512]{2,1,0:T(8,128)(2,1)} %convolution_convert_fusion.1) | copy-start | bytes 393220
  138.6 3.8 %copy-start.13 = (bf16[2,64,512]{2,1,0:T(8,128)(2,1)S(1)}, bf16[2,64,512]{2,1,0:T(8,128)(2,1)}, u32[]{:S(2)}) copy-start(bf16[2,64,512]{2,1,0:T(8,128)(2,1)} %convolution_convert_fusion.2) | copy-start | bytes 393220
  138.6 4.6 %copy-start.12 = (bf16[2,64,512]{2,1,0:T(8,128)(2,1)S(1)}, bf16[2,64,512]{2,1,0:T(8,128)(2,1)}, u32[]{:S(2)}) copy-start(bf16[2,64,512]{2,1,0:T(8,128)(2,1)} %convolution_convert_fusion.3) | copy-start | bytes 393220
  138.6 5.3 %copy-start.6 = (bf16[2,512,512]{1,2,0:T(8,128)(2,1)S(1)}, bf16[2,512,512]{1,2,0:T(8,128)(2,1)}, u32[]{:S(2)}) copy-start(bf16[2,512,512]{1,2,0:T(8,128)(2,1)} %get-tuple-element.75) | copy-start | bytes 3145732
  145.0 11.4 %copy-start.5 = (bf16[2,512,512]{1,2,0:T(8,128)(2,1)S(1)}, bf16[2,512,512]{1,2,0:T(8,128)(2,1)}, u32[]{:S(2)}) copy-start(bf16[2,512,512]{1,2,0:T(8,128)(2,1)} %get-tuple-element.79) | copy-start | bytes 3145732
  156.4 3.0 %copy-start.7 = (bf16[2,512,512]{1,2,0:T(8,128)(2,1)S(1)}, bf16[2,512,512]{1,2,0:T(8,128)(2,1)}, u32[]{:S(2)}) copy-start(bf16[2,512,512]{1,2,0:T(8,128)(2,1)} %get-tuple-element.77) | copy-start | bytes 3145732
  156.4 3.0 %copy-start.9 = (f32[2,512,64]{1,2,0:T(8,128)S(1)}, f32[2,512,64]{1,2,0:T(8,128)}, u32[]{:S(2)}) copy-start(f32[2,512,64]{1,2,0:T(8,128)} %fusion.118) | copy-start | bytes 786436
  156.4 3.0 %copy-start.20 = (bf16[512,128]{0,1:T(8,128)(2,1)S(1)}, bf16[512,128]{0,1:T(8,128)(2,1)}, u32[]{:S(2)}) copy-start(bf16[512,128]{0,1:T(8,128)(2,1)} %copy.127) | copy-start | bytes 393220
  162.3 14.7 %collective-permute-start.14 = (bf16[512,128]{1,0:T(8,128)(2,1)}, bf16[512,128]{1,0:T(8,128)(2,1)S(1)}, u32[]{:S(2)}, u32[]{:S(2)}) collective-permute-start(bf16[512,128]{1,0:T(8,128)(2,1)} %copy.145), channel_id=1, source_target_pairs={{0,1},{1,2},{2,3},{3,4},{4,5},{5,6},{6,7},{8,9},{9,10},{10,11},{11... | collective-permute-start | bytes 393224 | tf_op jit(solution)/shard_map/ppermute | solution.py:31
  164.4 14.6 %collective-permute-start.13 = (bf16[512,128]{1,0:T(8,128)(2,1)}, bf16[512,128]{1,0:T(8,128)(2,1)S(1)}, u32[]{:S(2)}, u32[]{:S(2)}) collective-permute-start(bf16[512,128]{1,0:T(8,128)(2,1)} %copy.143), channel_id=1, source_target_pairs={{1,0},{2,1},{3,2},{4,3},{5,4},{6,5},{7,6},{9,8},{10,9},{11,10},{12... | collective-permute-start | bytes 393224 | tf_op jit(solution)/shard_map/ppermute | solution.py:31
  168.2 15.6 %collective-permute-start.12 = (bf16[512,128]{1,0:T(8,128)(2,1)}, bf16[512,128]{1,0:T(8,128)(2,1)S(1)}, u32[]{:S(2)}, u32[]{:S(2)}) collective-permute-start(bf16[512,128]{1,0:T(8,128)(2,1)} %copy.140), channel_id=1, source_target_pairs={{2,0},{3,1},{4,2},{5,3},{6,4},{7,5},{10,8},{11,9},{12,10},{13,11},... | collective-permute-start | bytes 393224 | tf_op jit(solution)/shard_map/ppermute | solution.py:31
  170.6 16.7 %collective-permute-start.15 = (bf16[512,128]{1,0:T(8,128)(2,1)}, bf16[512,128]{1,0:T(8,128)(2,1)S(1)}, u32[]{:S(2)}, u32[]{:S(2)}) collective-permute-start(bf16[512,128]{1,0:T(8,128)(2,1)} %copy.147), channel_id=1, source_target_pairs={{0,2},{1,3},{2,4},{3,5},{4,6},{5,7},{8,10},{9,11},{10,12},{11,13},... | collective-permute-start | bytes 393224 | tf_op jit(solution)/shard_map/ppermute | solution.py:31
  174.6 13.4 %collective-permute-start.16 = (bf16[512,128]{1,0:T(8,128)(2,1)}, bf16[512,128]{1,0:T(8,128)(2,1)S(1)}, u32[]{:S(2)}, u32[]{:S(2)}) collective-permute-start(bf16[512,128]{1,0:T(8,128)(2,1)} %copy.150), channel_id=1, source_target_pairs={{2,0},{3,1},{4,2},{5,3},{6,4},{7,5},{10,8},{11,9},{12,10},{13,11},... | collective-permute-start | bytes 393224 | tf_op jit(solution)/shard_map/ppermute | solution.py:31
  177.0 11.0 %collective-permute-start.17 = (bf16[512,128]{1,0:T(8,128)(2,1)}, bf16[512,128]{1,0:T(8,128)(2,1)S(1)}, u32[]{:S(2)}, u32[]{:S(2)}) collective-permute-start(bf16[512,128]{1,0:T(8,128)(2,1)} %copy.153), channel_id=1, source_target_pairs={{1,0},{2,1},{3,2},{4,3},{5,4},{6,5},{7,6},{9,8},{10,9},{11,10},{12... | collective-permute-start | bytes 393224 | tf_op jit(solution)/shard_map/ppermute | solution.py:31
  178.9 9.1 %collective-permute-start.18 = (bf16[512,128]{1,0:T(8,128)(2,1)}, bf16[512,128]{1,0:T(8,128)(2,1)S(1)}, u32[]{:S(2)}, u32[]{:S(2)}) collective-permute-start(bf16[512,128]{1,0:T(8,128)(2,1)} %copy.155), channel_id=1, source_target_pairs={{0,1},{1,2},{2,3},{3,4},{4,5},{5,6},{6,7},{8,9},{9,10},{10,11},{11... | collective-permute-start | bytes 393224 | tf_op jit(solution)/shard_map/ppermute | solution.py:31
  183.8 7.1 %collective-permute-start.19 = (bf16[512,128]{1,0:T(8,128)(2,1)}, bf16[512,128]{1,0:T(8,128)(2,1)S(1)}, u32[]{:S(2)}, u32[]{:S(2)}) collective-permute-start(bf16[512,128]{1,0:T(8,128)(2,1)} %copy.157), channel_id=1, source_target_pairs={{0,2},{1,3},{2,4},{3,5},{4,6},{5,7},{8,10},{9,11},{10,12},{11,13},... | collective-permute-start | bytes 393224 | tf_op jit(solution)/shard_map/ppermute | solution.py:31
  (5 other events, 8.6 us)
Sparse Core Ops, SparseCore 0:
  86.6 16.0 all-gather.1
